TPU v7x, 128 devices: a whole 4x4x4 slice. The times are simulated.
128 devices in a mesh: src: 16 (over y, x), tgt: 8 (over z, core).
Axes of the slice: x: 4, y: 4, z: 4, core: 2. Of those that a mesh axis runs over, the one named last changes fastest.
Arguments:
- src_points: bfloat16 [32768, 1024], P(('src', 'tgt')), may hold values from -6 to 6
- tgt_points: bfloat16 [32768, 1024], P(('src', 'tgt')), may hold values from -24 to 24
- src_factor: bfloat16 [32768, 256], P(('src', 'tgt')), may hold values from 0.25 to 4
- tgt_factor: bfloat16 [32768, 256], P(('src', 'tgt')), may hold values from 0.25 to 4
- inner_marginal: float32 [256], replicated, may hold values from 0.3 to 3
- src_cluster: int32 [32768], P(('src', 'tgt')), may hold values from 0 to 255, as said below
- tgt_cluster: int32 [32768], P(('src', 'tgt')), may hold values from 0 to 255, as said below
Outputs:
- src_update: bfloat16 [32768, 256], P(('src', 'tgt'))
- tgt_update: bfloat16 [32768, 256], P(('src', 'tgt'))
- mapped: bfloat16 [32768, 1024], P(('src', 'tgt'))
Inputs may be any that keep to these rules, and one draw needn't show every extreme that they name: `src_cluster`: Co-cluster c belongs to the owner c // 2 (devices in the order of src+tgt). Over the 256 source points of one device, the points whose co-cluster belongs to one owner number at most 4, and at least one for every owner; some owner receives exactly 4 from every device. `tgt_cluster`: Co-cluster c belongs to the owner c // 2. Over the 256 target points of one device, the points whose co-cluster belongs to one owner number at most 4, and at least one for every owner; some owner receives exactly 4 from every device. Every co-cluster holds at least one target point.
All inputs are finite; a program needn't handle non-finite values. Where the computation divides by a largest or mean magnitude, that divisor is 1e-20 or more.
Results may differ from a plain program's by a relative error of at most 0.0049.
Values may be sent and summed in bfloat16 or wider, within the bound.
A program may use at most 64 MiB of HBM per device.

v0:
```python
import math

import jax
import jax.numpy as jnp
from jax import lax
from jax.sharding import PartitionSpec as P

CL_DEV = 2


GAMMA = 2.0
TEMPER = 0.03
EPS = 1e-06


def contract_rows(left, right):
    return lax.dot_general(
        left, right, (((0,), (0,)), ((), ())), preferred_element_type=jnp.float32
    )


def mirror_step(points, total_round, factor, inner_marginal):
    gradient = (
        -jnp.dot(points, total_round, preferred_element_type=jnp.float32) / inner_marginal[None, :]
    )
    row_scale = jnp.max(jnp.abs(gradient), axis=1, keepdims=True) + EPS
    tilted = factor.astype(jnp.float32) * jnp.exp(-GAMMA * gradient / row_scale)
    return (tilted / jnp.mean(tilted, axis=1, keepdims=True)).astype(jnp.bfloat16)


def pack_rows(points, factor, cluster, n_dev, capacity, empty_label):
    row_count = points.shape[0]
    owners = cluster // CL_DEV
    onehot = (owners[:, None] == jnp.arange(n_dev, dtype=jnp.int32)[None, :]).astype(jnp.bfloat16)
    triangle = (jnp.arange(row_count)[:, None] > jnp.arange(row_count)[None, :]).astype(
        jnp.bfloat16
    )
    earlier = jnp.dot(triangle, onehot, preferred_element_type=jnp.float32)
    ranking = jnp.sum(earlier * onehot.astype(jnp.float32), axis=1).astype(jnp.int32)
    slot_index = owners * capacity + ranking
    buffer_len = n_dev * capacity
    moved_rows = jnp.zeros((buffer_len, points.shape[1]), jnp.bfloat16).at[slot_index].set(points)
    carried = jnp.zeros((buffer_len, factor.shape[1]), jnp.bfloat16).at[slot_index].set(factor)
    labels = jnp.full((buffer_len,), empty_label, jnp.int32).at[slot_index].set(cluster)
    return (slot_index, moved_rows, carried, labels)


def owner_maps(src_rows, src_carried, src_labels, tgt_rows, tgt_carried, tgt_labels):
    factor_width = src_carried.shape[1]
    buffer_len = src_rows.shape[0]
    inv_src = lax.rsqrt(jnp.sum(jnp.square(src_rows.astype(jnp.float32)), axis=1) + EPS)
    inv_tgt = lax.rsqrt(jnp.sum(jnp.square(tgt_rows.astype(jnp.float32)), axis=1) + EPS)
    block_len = math.gcd(buffer_len, 512)
    n_blocks = buffer_len // block_len

    def one_block(pieces):
        rows_block, carried_block, labels_block, inv_block = pieces
        products = lax.dot_general(
            rows_block, tgt_rows, (((1,), (1,)), ((), ())), preferred_element_type=jnp.float32
        )
        cosine = products * inv_block[:, None] * inv_tgt[None, :]
        weight = (
            lax.dot_general(
                carried_block,
                tgt_carried,
                (((1,), (1,)), ((), ())),
                preferred_element_type=jnp.float32,
            )
            / factor_width
        )
        kernel = jnp.where(
            labels_block[:, None] == tgt_labels[None, :],
            weight * jnp.exp((cosine - 1.0) / TEMPER),
            0.0,
        )
        denominator = jnp.sum(kernel, axis=1, keepdims=True)
        denominator = jnp.where(denominator > 0, denominator, 1.0)
        transport = (kernel / denominator).astype(jnp.bfloat16)
        return jnp.dot(transport, tgt_rows, preferred_element_type=jnp.float32).astype(jnp.bfloat16)

    images = lax.map(
        one_block,
        (
            src_rows.reshape(n_blocks, block_len, src_rows.shape[1]),
            src_carried.reshape(n_blocks, block_len, factor_width),
            src_labels.reshape(n_blocks, block_len),
            inv_src.reshape(n_blocks, block_len),
        ),
    )
    return images.reshape(buffer_len, src_rows.shape[1])


def per_device(
    src_points, tgt_points, src_factor, tgt_factor, inner_marginal, src_cluster, tgt_cluster
):
    n_src = lax.axis_size("src")
    n_tgt = lax.axis_size("tgt")
    n_dev = n_src * n_tgt
    capacity = 2 * src_points.shape[0] // n_dev
    tgt_part = contract_rows(tgt_points, tgt_factor)
    src_part = contract_rows(src_points, src_factor)
    tgt_total, src_total = lax.psum((tgt_part, src_part), ("src", "tgt"))
    tgt_round = tgt_total.astype(jnp.bfloat16)
    src_round = src_total.astype(jnp.bfloat16)
    src_update = mirror_step(src_points, tgt_round, src_factor, inner_marginal)
    tgt_update = mirror_step(tgt_points, src_round, tgt_factor, inner_marginal)
    src_slot, src_rows, src_carried, src_labels = pack_rows(
        src_points, src_update, src_cluster, n_dev, capacity, -2
    )
    tgt_slot, tgt_rows, tgt_carried, tgt_labels = pack_rows(
        tgt_points, tgt_update, tgt_cluster, n_dev, capacity, -1
    )
    arrived = (
        lax.all_to_all(src_rows, ("src", "tgt"), split_axis=0, concat_axis=0, tiled=True),
        lax.all_to_all(src_carried, ("src", "tgt"), split_axis=0, concat_axis=0, tiled=True),
        lax.all_to_all(src_labels, ("src", "tgt"), split_axis=0, concat_axis=0, tiled=True),
        lax.all_to_all(tgt_rows, ("src", "tgt"), split_axis=0, concat_axis=0, tiled=True),
        lax.all_to_all(tgt_carried, ("src", "tgt"), split_axis=0, concat_axis=0, tiled=True),
        lax.all_to_all(tgt_labels, ("src", "tgt"), split_axis=0, concat_axis=0, tiled=True),
    )
    images = owner_maps(arrived[0], arrived[1], arrived[2], arrived[3], arrived[4], arrived[5])
    returned = lax.all_to_all(images, ("src", "tgt"), split_axis=0, concat_axis=0, tiled=True)
    mapped = returned[src_slot]
    return (src_update, tgt_update, mapped)


def solution(mesh):
    placed = (
        P(("src", "tgt"), None),
        P(("src", "tgt"), None),
        P(("src", "tgt"), None),
        P(("src", "tgt"), None),
        P(),
        P(("src", "tgt")),
        P(("src", "tgt")),
    )
    return jax.shard_map(
        per_device,
        mesh=mesh,
        in_specs=placed,
        out_specs=(P(("src", "tgt"), None), P(("src", "tgt"), None), P(("src", "tgt"), None)),
        check_vma=False,
    )
```

profile of v0, /device:TPU:1, one launch (start us, length us, event | category | flops | bytes accessed | tf_op | source)
XLA Modules:
  0.0 229.4 jit_solution(13507849118206767590)
XLA Ops:
  0.6 0.7 and_select_fusion
  1.3 0.2 fusion.9
  1.6 0.7 compare_select_fusion.1
  2.3 1.6 scatter_custom_fusion.1
  3.8 0.7 all_to_all.54
  4.5 11.5 %all-to-all-start.1 = ((s32[128,4,1]{1,2,0:T(1,128)}), s32[128,4,1]{1,2,0:T(1,128)S(1)}, u32[]{:S(2)}, u32[]{:S(2)}) async-start(s32[128,4,1]{1,2,0:T(1,128)} %bitcast.3), calls=%async_computation.1 | async-start | bytes 131072 | tf_op jit(solution)/shard_map/all_to_all | solution.py:119
  16.0 1.0 copy.21
  17.1 1.5 fusion.32
  18.5 0.1 copy.20
  18.7 0.4 fusion.33
  19.0 77.9 %all-reduce.2 = (bf16[1024,256]{1,0:T(8,128)(2,1)}, bf16[1024,256]{1,0:T(8,128)(2,1)}) all-reduce(f32[1024,256]{1,0:T(8,128)S(1)} %fusion.32, f32[1024,256]{1,0:T(8,128)S(1)} %fusion.33), channel_id=1, replica_groups=mesh['src'=16,'tgt'=8] {'src','tgt'}, use_global_device_ids=true, to_apply=%region_0.0 | all-reduce | flops 524288 | bytes 3145728 | tf_op jit(solution)/shard_map/psum | solution.py:102
  96.9 1.5 abs_reduce_fusion.1
  98.4 0.0 copy-start.6
  98.5 0.4 abs_reduce_fusion
  98.8 0.3 copy-done.6
  99.1 0.2 fusion.8
  99.4 0.1 fusion.29
  99.6 1.4 scatter_custom_fusion
  101.0 0.7 all_to_all.52
  101.7 5.8 %all-to-all-start = ((s32[128,4,1]{1,2,0:T(1,128)}), s32[128,4,1]{1,2,0:T(1,128)S(1)}, u32[]{:S(2)}, u32[]{:S(2)}) async-start(s32[128,4,1]{1,2,0:T(1,128)} %bitcast.2), calls=%async_computation | async-start | bytes 131072 | tf_op jit(solution)/shard_map/all_to_all | solution.py:116
  107.5 0.1 divide_convert_fusion.3
  107.6 0.1 copy.26
  107.7 0.0 copy-start.4
  107.7 1.5 scatter_custom_fusion.2
  109.2 0.8 all_to_all.56
  110.0 6.9 %all-to-all-done = s32[128,4,1]{1,2,0:T(1,128)S(1)} async-done(((s32[128,4,1]{1,2,0:T(1,128)}), s32[128,4,1]{1,2,0:T(1,128)S(1)}, u32[]{:S(2)}, u32[]{:S(2)}) %all-to-all-start) | async-done | bytes 2080 | tf_op jit(solution)/shard_map/all_to_all | solution.py:116
  116.9 4.6 %all-to-all-start.2 = ((bf16[128,4,256]{2,1,0:T(4,128)(2,1)}), bf16[128,4,256]{2,1,0:T(4,128)(2,1)S(1)}, u32[]{:S(2)}, u32[]{:S(2)}) async-start(bf16[128,4,256]{2,1,0:T(4,128)(2,1)} %all_to_all.56), calls=%async_computation.2 | async-start | bytes 524288 | tf_op jit(solution)/shard_map/all_to_all | solution.py:115
  121.5 0.1 divide_convert_fusion.2
  121.6 0.1 copy.27
  121.7 1.5 scatter_custom_fusion.3
  123.3 0.8 all_to_all.59
  124.1 8.5 %all-to-all-done.2 = bf16[128,4,256]{2,1,0:T(4,128)(2,1)S(1)} async-done(((bf16[128,4,256]{2,1,0:T(4,128)(2,1)}), bf16[128,4,256]{2,1,0:T(4,128)(2,1)S(1)}, u32[]{:S(2)}, u32[]{:S(2)}) %all-to-all-start.2) | async-done | bytes 262176 | tf_op jit(solution)/shard_map/all_to_all | solution.py:115
  132.5 4.5 %all-to-all-start.3 = ((bf16[128,4,256]{2,1,0:T(4,128)(2,1)}), bf16[128,4,256]{2,1,0:T(4,128)(2,1)S(1)}, u32[]{:S(2)}, u32[]{:S(2)}) async-start(bf16[128,4,256]{2,1,0:T(4,128)(2,1)} %all_to_all.59), calls=%async_computation.3 | async-start | bytes 524288 | tf_op jit(solution)/shard_map/all_to_all | solution.py:118
  137.1 1.9 scatter_custom_fusion.5
  139.0 1.2 all_to_all.65
  140.2 7.8 %all-to-all-done.3 = bf16[128,4,256]{2,1,0:T(4,128)(2,1)S(1)} async-done(((bf16[128,4,256]{2,1,0:T(4,128)(2,1)}), bf16[128,4,256]{2,1,0:T(4,128)(2,1)S(1)}, u32[]{:S(2)}, u32[]{:S(2)}) %all-to-all-start.3) | async-done | bytes 262176 | tf_op jit(solution)/shard_map/all_to_all | solution.py:118
  148.1 4.5 %all-to-all-start.5 = ((bf16[128,4,1024]{2,1,0:T(4,128)(2,1)}), bf16[128,4,1024]{2,1,0:T(4,128)(2,1)S(1)}, u32[]{:S(2)}, u32[]{:S(2)}) async-start(bf16[128,4,1024]{2,1,0:T(4,128)(2,1)} %all_to_all.65), calls=%async_computation.5 | async-start | bytes 2097152 | tf_op jit(solution)/shard_map/all_to_all | solution.py:117
  152.6 1.9 scatter_custom_fusion.4
  154.5 1.2 all_to_all.62
  155.7 16.0 %all-to-all-done.5 = bf16[128,4,1024]{2,1,0:T(4,128)(2,1)S(1)} async-done(((bf16[128,4,1024]{2,1,0:T(4,128)(2,1)}), bf16[128,4,1024]{2,1,0:T(4,128)(2,1)S(1)}, u32[]{:S(2)}, u32[]{:S(2)}) %all-to-all-start.5) | async-done | bytes 1048608 | tf_op jit(solution)/shard_map/all_to_all | solution.py:117
  171.7 4.7 %all-to-all-start.4 = ((bf16[128,4,1024]{2,1,0:T(4,128)(2,1)}), bf16[128,4,1024]{2,1,0:T(4,128)(2,1)S(1)}, u32[]{:S(2)}, u32[]{:S(2)}) async-start(bf16[128,4,1024]{2,1,0:T(4,128)(2,1)} %all_to_all.62), calls=%async_computation.4 | async-start | bytes 2097152 | tf_op jit(solution)/shard_map/all_to_all | solution.py:114
  176.5 0.5 broadcast.165
  177.0 0.8 reduce.11
  177.8 0.1 eq.58
  177.9 0.8 reduce.10
  178.7 0.1 eq.53
  178.8 0.1 all_to_all.58
  178.9 0.8 all_to_all.61
  179.7 1.3 convolution_multiply_fusion.1
  181.0 0.6 multiply_reduce_fusion
  181.6 0.1 rsqrt.19
  181.7 13.9 %all-to-all-done.4 = bf16[128,4,1024]{2,1,0:T(4,128)(2,1)S(1)} async-done(((bf16[128,4,1024]{2,1,0:T(4,128)(2,1)}), bf16[128,4,1024]{2,1,0:T(4,128)(2,1)S(1)}, u32[]{:S(2)}, u32[]{:S(2)}) %all-to-all-start.4) | async-done | bytes 1048608 | tf_op jit(solution)/shard_map/all_to_all | solution.py:114
  195.6 0.6 multiply_reduce_fusion.1
  196.3 0.1 rsqrt.17
  196.4 1.1 all_to_all.67
  197.5 1.2 all_to_all.64
  198.7 0.4 copy-done
  199.1 2.2 fusion.31
  201.3 0.7 convolution_convert_fusion
  202.1 1.2 all_to_all.68
  203.3 4.7 %all-to-all-start.6 = ((bf16[128,4,1024]{2,1,0:T(4,128)(2,1)}), bf16[128,4,1024]{2,1,0:T(4,128)(2,1)S(1)}, u32[]{:S(2)}, u32[]{:S(2)}) async-start(bf16[128,4,1024]{2,1,0:T(4,128)(2,1)} %all_to_all.68), calls=%async_computation.6 | async-start | bytes 2097152 | tf_op jit(solution)/shard_map/all_to_all | solution.py:122
  208.0 19.1 %all-to-all-done.6 = bf16[128,4,1024]{2,1,0:T(4,128)(2,1)S(1)} async-done(((bf16[128,4,1024]{2,1,0:T(4,128)(2,1)}), bf16[128,4,1024]{2,1,0:T(4,128)(2,1)S(1)}, u32[]{:S(2)}, u32[]{:S(2)}) %all-to-all-start.6) | async-done | bytes 1048608 | tf_op jit(solution)/shard_map/all_to_all | solution.py:122
  227.2 0.3 all_to_all.70
  227.5 2.0 gather_fusion
  (25 shorter events, 0.1 us)
Async XLA Ops:
  4.5 14.0 %copy-start.3 = (bf16[256,256]{1,0:T(8,128)(2,1)S(1)}, bf16[256,256]{1,0:T(8,128)(2,1)}, u32[]{:S(2)}) copy-start(bf16[256,256]{1,0:T(8,128)(2,1)} %param.9) | copy-start | bytes 393220
  4.5 97.1 %all-to-all-start.1 = ((s32[128,4,1]{1,2,0:T(1,128)}), s32[128,4,1]{1,2,0:T(1,128)S(1)}, u32[]{:S(2)}, u32[]{:S(2)}) async-start(s32[128,4,1]{1,2,0:T(1,128)} %bitcast.3), calls=%async_computation.1 | async-start | bytes 131072 | tf_op jit(solution)/shard_map/all_to_all | solution.py:119
  17.1 1.6 copy-start.2
  19.0 77.9 %copy-start.8 = (f32[256]{0:T(256)S(1)}, f32[256]{0:T(256)}, u32[]{:S(2)}) copy-start(f32[256]{0:T(256)} %param.11) | copy-start | bytes 3076
  96.9 1.5 copy-start.1
  96.9 1.5 copy-start.7
  98.4 0.7 copy-start.6
  101.7 15.2 %all-to-all-start = ((s32[128,4,1]{1,2,0:T(1,128)}), s32[128,4,1]{1,2,0:T(1,128)S(1)}, u32[]{:S(2)}, u32[]{:S(2)}) async-start(s32[128,4,1]{1,2,0:T(1,128)} %bitcast.2), calls=%async_computation | async-start | bytes 131072 | tf_op jit(solution)/shard_map/all_to_all | solution.py:116
  107.7 14.0 %copy-start.4 = (bf16[256,256]{1,0:T(8,128)(2,1)}, bf16[256,256]{1,0:T(8,128)(2,1)S(1)}, u32[]{:S(2)}) copy-start(bf16[256,256]{1,0:T(8,128)(2,1)S(1)} %copy.26) | copy-start | bytes 393220
  116.9 15.6 %all-to-all-start.2 = ((bf16[128,4,256]{2,1,0:T(4,128)(2,1)}), bf16[128,4,256]{2,1,0:T(4,128)(2,1)S(1)}, u32[]{:S(2)}, u32[]{:S(2)}) async-start(bf16[128,4,256]{2,1,0:T(4,128)(2,1)} %all_to_all.56), calls=%async_computation.2 | async-start | bytes 524288 | tf_op jit(solution)/shard_map/all_to_all | solution.py:115
  121.7 10.8 %copy-start.5 = (bf16[256,256]{1,0:T(8,128)(2,1)}, bf16[256,256]{1,0:T(8,128)(2,1)S(1)}, u32[]{:S(2)}) copy-start(bf16[256,256]{1,0:T(8,128)(2,1)S(1)} %copy.27) | copy-start | bytes 393220
  132.5 15.5 %all-to-all-start.3 = ((bf16[128,4,256]{2,1,0:T(4,128)(2,1)}), bf16[128,4,256]{2,1,0:T(4,128)(2,1)S(1)}, u32[]{:S(2)}, u32[]{:S(2)}) async-start(bf16[128,4,256]{2,1,0:T(4,128)(2,1)} %all_to_all.59), calls=%async_computation.3 | async-start | bytes 524288 | tf_op jit(solution)/shard_map/all_to_all | solution.py:118
  148.1 23.7 %all-to-all-start.5 = ((bf16[128,4,1024]{2,1,0:T(4,128)(2,1)}), bf16[128,4,1024]{2,1,0:T(4,128)(2,1)S(1)}, u32[]{:S(2)}, u32[]{:S(2)}) async-start(bf16[128,4,1024]{2,1,0:T(4,128)(2,1)} %all_to_all.65), calls=%async_computation.5 | async-start | bytes 2097152 | tf_op jit(solution)/shard_map/all_to_all | solution.py:117
  171.7 23.9 %all-to-all-start.4 = ((bf16[128,4,1024]{2,1,0:T(4,128)(2,1)}), bf16[128,4,1024]{2,1,0:T(4,128)(2,1)S(1)}, u32[]{:S(2)}, u32[]{:S(2)}) async-start(bf16[128,4,1024]{2,1,0:T(4,128)(2,1)} %all_to_all.62), calls=%async_computation.4 | async-start | bytes 2097152 | tf_op jit(solution)/shard_map/all_to_all | solution.py:114
  197.5 1.6 copy-start
  203.3 23.9 %all-to-all-start.6 = ((bf16[128,4,1024]{2,1,0:T(4,128)(2,1)}), bf16[128,4,1024]{2,1,0:T(4,128)(2,1)S(1)}, u32[]{:S(2)}, u32[]{:S(2)}) async-start(bf16[128,4,1024]{2,1,0:T(4,128)(2,1)} %all_to_all.68), calls=%async_computation.6 | async-start | bytes 2097152 | tf_op jit(solution)/shard_map/all_to_all | solution.py:122
where the time goes:
time: 230 us; the launch traced here: 229 us
  blocking collectives  77.9 us (34%)
  waiting for transfers between devices  72.3 us (31%)
  starting transfers between devices  40.3 us (18%)
  local copies, waits for them, and re-layouts  24.9 us (11%)
  matrix products  8.35 us (4%)
  other arithmetic  4.6 us (2%)
    psum x1, blocking collectives, per_device(): tgt_total, src_total = lax.psum((tgt_part, src_part), ('src', 'tgt'))  77.9 us
    all_to_all x1, waiting for transfers between devices, per_device(): lax.all_to_all(images, ('src', 'tgt'), split_axis=0, concat_axis=0, tiled...  19.1 us
    all_to_all x1, waiting for transfers between devices, per_device(): lax.all_to_all(tgt_rows, ('src', 'tgt'), split_axis=0, concat_axis=0, til...  16 us
    all_to_all x1, waiting for transfers between devices, per_device(): lax.all_to_all(src_rows, ('src', 'tgt'), split_axis=0, concat_axis=0, til...  13.9 us
    all_to_all x1, starting transfers between devices, per_device(): lax.all_to_all(tgt_labels, ('src', 'tgt'), split_axis=0, concat_axis=0, t...  11.5 us
    all_to_all x1, waiting for transfers between devices, per_device(): lax.all_to_all(src_carried, ('src', 'tgt'), split_axis=0, concat_axis=0,...  8.47 us
    all_to_all x1, waiting for transfers between devices, per_device(): lax.all_to_all(tgt_carried, ('src', 'tgt'), split_axis=0, concat_axis=0,...  7.85 us
    all_to_all x1, waiting for transfers between devices, per_device(): lax.all_to_all(src_labels, ('src', 'tgt'), split_axis=0, concat_axis=0, t...  6.91 us
  transfers between devices with their start and end apart: 7, of which 6 were waited for; matrix products, arithmetic and copies ran while one was open for 8% of the time, Pallas kernels for 0%

commit v1 on v0

v1 whole, which is shorter than its diff:
```python
import jax
import jax.numpy as jnp
from jax import lax
from jax.experimental import pallas as pl
from jax.experimental.pallas import tpu as pltpu
from jax.sharding import PartitionSpec as P

CL_DEV = 2
CAP = 4
GAMMA = 2.0
TEMPER = 0.03
EPS = 1e-06

D = 1024
R = 256
ROWS = 256
NDEV = 128
SLOTS = NDEV * CAP
QUART = D // 4
GROUP = 16
NGROUP = NDEV // GROUP
MESH = pl.DeviceIdType.MESH
BF = jnp.bfloat16
F32 = jnp.float32
I32 = jnp.int32


def offset_of(k):
    x1, y1, z1, x0, y0, z0, c = ((k >> b) & 1 for b in (6, 5, 4, 3, 2, 1, 0))
    return (y1 * 8 + y0 * 4 + x1 * 2 + x0, z1 * 4 + z0 * 2 + c)


def hops(k):
    ds, dt = offset_of(k)
    ring = (0, 1, 2, 1)
    return ring[ds // 4] + ring[ds % 4] + ring[dt // 2]


def place_of(owner):
    bit = lambda b: (owner // (1 << b)) % 2
    y1, y0, x1, x0, z1, z0, c = (bit(b) for b in (6, 5, 4, 3, 2, 1, 0))
    return x1 * 64 + y1 * 32 + z1 * 16 + x0 * 8 + y0 * 4 + z0 * 2 + c


def flips(value, bits):
    parts = [(value // (1 << b)) % 2 for b in range(bits)]
    out = []
    for m in range(1 << bits):
        total = 0
        for b in range(bits):
            total = total + ((1 - parts[b]) if (m >> b) & 1 else parts[b]) * (1 << b)
        out.append(total)
    return out


def dot(a, b, dims=((1,), (0,)), precision=None):
    return lax.dot_general(a, b, (dims, ((), ())), preferred_element_type=F32, precision=precision)


def iota(shape, axis):
    return lax.broadcasted_iota(I32, shape, axis)


def mirror(points, total_t, factor, marginal):
    gradient = dot(points, total_t, ((1,), (1,))) / marginal
    row_scale = jnp.max(jnp.abs(gradient), axis=1, keepdims=True) + EPS
    tilted = factor.astype(F32) * jnp.exp(GAMMA * gradient / row_scale)
    mean = jnp.mean(tilted, axis=1, keepdims=True)
    return (tilted / jnp.where(mean > 0, mean, 1.0)).astype(BF)


def slots_of(cluster_row, me_bits):
    eye = iota((ROWS, ROWS), 0) == iota((ROWS, ROWS), 1)
    owner_row = cluster_row // CL_DEV
    cluster_col = jnp.sum(jnp.where(eye, cluster_row, 0).astype(F32), axis=1, keepdims=True).astype(I32)
    owner_col = cluster_col // CL_DEV
    same = owner_col == owner_row
    below = iota((ROWS, ROWS), 0) < iota((ROWS, ROWS), 1)
    above = iota((ROWS, ROWS), 1) < iota((ROWS, ROWS), 0)
    rank_row = jnp.sum(jnp.where(same & below, 1.0, 0.0), axis=0, keepdims=True).astype(I32)
    rank_col = jnp.sum(jnp.where(same & above, 1.0, 0.0), axis=1, keepdims=True).astype(I32)

    def block(owner):
        place = place_of(owner)
        total = 0
        for b in range(7):
            mine = me_bits[b]
            theirs = (place // (1 << b)) % 2
            total = total + (mine + theirs - 2 * mine * theirs) * (1 << b)
        return total

    return block(owner_row), rank_row, block(owner_col), rank_col, cluster_col


def kernel(
    sp, tp, sf, tf, marg, scl, tcl,
    su, tu, mp,
    pf, pp, rx, cs, rr, mm, ts, tr, ss, sr, ls, lr, tall, ball, sfall, irow, lcol, lrow, isend, irecv,
    pair_s, pair_r, rs_s, rs_r, ag_s, ag_r, pb_s, pb_r, lab_s, lab_r, tg_s, tg_r, sc_s, sc_r, rt_s, rt_r,
):
    s = lax.axis_index("src")
    t = lax.axis_index("tgt")
    z = t // 2
    core = t % 2
    sx = flips(s, 4)
    tx = flips(t, 3)
    zx = flips(z, 2)

    def peer(k):
        ds, dt = offset_of(k)
        return (sx[ds], tx[dt])

    partner = (s, tx[1])

    barrier = pltpu.get_barrier_semaphore()
    for k in range(1, NDEV):
        pl.semaphore_signal(barrier, inc=1, device_id=peer(k), device_id_type=MESH)

    part = dot(tf[...], tp[...], ((0,), (0,)))
    pf[0] = part
    pp[0] = part.astype(BF)
    part = dot(sf[...], sp[...], ((0,), (0,)))
    pf[1] = part
    pp[1] = part.astype(BF)

    me = s * 8 + t
    mp_place = place_of(me)
    me_bits = [(mp_place // (1 << b)) % 2 for b in range(7)]
    s_blk_row, s_rank_row, s_blk_col, s_rank_col, s_cl_col = slots_of(scl[...], me_bits)
    t_blk_row, t_rank_row, t_blk_col, t_rank_col, t_cl_col = slots_of(tcl[...], me_bits)
    s_slot_row = s_blk_row * CAP + s_rank_row
    t_slot_row = t_blk_row * CAP + t_rank_row
    s_slot_col = s_blk_col * CAP + s_rank_col

    lane = iota((ROWS, NDEV), 1)
    blk = iota((NDEV, ROWS), 0)
    s_val = jnp.where(lane == s_rank_col, (s_cl_col % CL_DEV + 1).astype(F32), 0.0).astype(BF)
    t_val = jnp.where(lane == t_rank_col + CAP, (t_cl_col % CL_DEV + 1).astype(F32), 0.0).astype(BF)
    s_hot = jnp.where(blk == s_blk_row, 1.0, 0.0).astype(BF)
    t_hot = jnp.where(blk == t_blk_row, 1.0, 0.0).astype(BF)
    labels = (dot(s_hot, s_val) + dot(t_hot, t_val)).astype(I32)
    ls[...] = labels.reshape(NDEV, 1, NDEV)

    row = iota((ROWS, ROWS), 0)
    col = iota((ROWS, ROWS), 1)
    to_wire = jnp.where(col == (row // 4 % 4) * 64 + (row // 16) * 4 + row % 4, 1.0, 0.0).astype(BF)
    from_wire = jnp.where(row == (col // 4 % 4) * 64 + (col // 16) * 4 + col % 4, 1.0, 0.0).astype(BF)

    def hot_rows(b, slot_row):
        return jnp.where(iota((64, ROWS), 0) + b * 64 == slot_row, 1.0, 0.0).astype(BF)

    def quarters(x):
        return jnp.concatenate([x[:, q * QUART : (q + 1) * QUART] for q in range(4)], axis=0)

    def pack_tgt(b, carry):
        t_sel = hot_rows(b, t_slot_row)
        s_sel = hot_rows(b, s_slot_row)
        rows = dot(t_sel, tp[...]).astype(BF)
        f_t = dot(t_sel, tf[...]).astype(BF)
        f_s = dot(s_sel, sf[...]).astype(BF)
        facs = jnp.concatenate([f_s[:, :128], f_s[:, 128:], f_t[:, :128], f_t[:, 128:]], axis=0)
        at = pl.ds(pl.multiple_of(b * 256, 256), 256)
        ts[at, 0:QUART] = dot(to_wire, quarters(rows)).astype(BF)
        ts[at, QUART : QUART + 128] = dot(to_wire, facs).astype(BF)
        return carry

    def pack_src(b, carry):
        rows = dot(hot_rows(b, s_slot_row), sp[...]).astype(BF)
        at = pl.ds(pl.multiple_of(b * 256, 256), 256)
        ss[at, :] = dot(to_wire, quarters(rows)).astype(BF)
        return carry

    lax.fori_loop(0, NGROUP, pack_tgt, 0)

    pl.semaphore_wait(barrier, NDEV - 1)

    def remote(src, dst, send, recv, device):
        return pltpu.make_async_remote_copy(
            src_ref=src, dst_ref=dst, send_sem=send, recv_sem=recv, device_id=device, device_id_type=MESH
        )

    pair = remote(pp.at[1 - core], rx, pair_s, pair_r, partner)
    pair.start()

    lax.fori_loop(0, NGROUP, pack_src, 0)
    tr[0:16, :] = ts[0:16, :]
    sr[0:16, :] = ss[0:16, :]
    lr[0] = ls[0]

    pair.wait_recv()
    cs[...] = (pf[core] + rx[...].astype(F32)).astype(BF)

    for kc in range(1, 64):
        ds, dz = kc // 4, kc % 4
        remote(
            cs.at[pl.ds(pl.multiple_of(sx[ds] * 16, 16), 16), pl.ds(pl.multiple_of(zx[dz] * 256, 256), 256)],
            rr.at[kc], rs_s, rs_r, (sx[ds], tx[dz * 2]),
        ).start()

    order = sorted(range(1, NDEV), key=lambda k: (-(k // GROUP), -hops(k)))
    for k in order:
        at = pl.ds(k * 16, 16)
        remote(ts.at[at], tr.at[at], tg_s, tg_r, peer(k)).start()
        remote(ls.at[k], lr.at[k], lab_s, lab_r, peer(k)).start()

    rest = rr.at[pl.ds(1, 63)]
    remote(rest, rest, rs_s, rs_r, partner).wait_recv()
    my_rows = pl.ds(pl.multiple_of(s * 16, 16), 16)
    my_cols = pl.ds(pl.multiple_of(z * 256, 256), 256)
    total = cs[my_rows, my_cols].astype(F32)
    for kc in range(1, 64):
        total = total + rr[kc].astype(F32)
    mm[core, my_rows, my_cols] = total.astype(BF)

    mine = mm.at[core, my_rows, my_cols]
    for kc in range(1, 64):
        ds, dz = kc // 4, kc % 4
        remote(mine, mine, ag_s, ag_r, (sx[ds], tx[dz * 2])).start()
    for k in order:
        at = pl.ds(k * 16, 16)
        g = k // GROUP
        remote(ss.at[at], sr.at[at], sc_s.at[g], sc_r.at[g], peer(k)).start()
    remote(rest, rest, ag_s, ag_r, partner).wait_recv()
    pair_back = remote(mm.at[core], mm.at[core], pb_s, pb_r, partner)
    pair_back.start()
    remote(mm.at[1 - core], mm.at[1 - core], pb_s, pb_r, partner).wait_recv()

    marginal = marg[...]
    su[...] = mirror(sp[...], mm[0], sf[...], marginal)
    tu[...] = mirror(tp[...], mm[1], tf[...], marginal)

    tgt_rest = pl.ds(16, 2032)
    remote(ts.at[tgt_rest], tr.at[tgt_rest], tg_s, tg_r, partner).wait_recv()
    lab_rest = pl.ds(1, 127)
    remote(ls.at[lab_rest], lr.at[lab_rest], lab_s, lab_r, partner).wait_recv()

    def owner_tgt(b, carry):
        at = pl.ds(pl.multiple_of(b * 256, 256), 256)
        to = pl.ds(pl.multiple_of(b * 64, 64), 64)
        rows = dot(from_wire, tr[at, 0:QUART]).astype(BF)
        facs = dot(from_wire, tr[at, QUART : QUART + 128]).astype(BF)
        points = jnp.concatenate([rows[q * 64 : (q + 1) * 64] for q in range(4)], axis=1)
        tall[to, :] = points
        sfall[to, :] = jnp.concatenate([facs[0:64], facs[64:128]], axis=1)
        tgt_fac = jnp.concatenate([facs[128:192], facs[192:256]], axis=1)
        ball[to, :] = mirror(points, mm[1], tgt_fac, marginal)
        return carry

    lax.fori_loop(0, NGROUP, owner_tgt, 0)

    squares = jnp.zeros((SLOTS, 128), F32)
    for j in range(D // 128):
        piece = tall[:, j * 128 : (j + 1) * 128].astype(F32)
        squares = squares + piece * piece
    ones = jnp.ones((8, 128), F32)
    sums = dot(ones, squares, ((1,), (1,)), precision=lax.Precision.HIGHEST)
    irow[...] = lax.rsqrt(sums + EPS)

    got = lr[...].reshape(NDEV, NDEV).astype(F32).astype(BF)
    spread = jnp.where(iota((SLOTS, NDEV), 0) // CAP == iota((SLOTS, NDEV), 1), 1.0, 0.0).astype(BF)
    per_slot = dot(spread, got)
    slot_lane = iota((SLOTS, NDEV), 1) - iota((SLOTS, NDEV), 0) % CAP
    lcol[...] = jnp.broadcast_to(
        jnp.sum(jnp.where(slot_lane == 0, per_slot, 0.0), axis=1, keepdims=True), (SLOTS, NDEV)
    )
    tgt_lab = jnp.where(slot_lane == CAP, per_slot, 0.0).astype(BF)
    lrow[...] = dot(jnp.ones((8, NDEV), BF), tgt_lab, ((1,), (1,)))

    STEP = 2
    span = 64 * STEP

    def owner_src(first):
        at0 = first * 64
        pieces = []
        for j in range(STEP):
            at = slice((first + j) * 256, (first + j + 1) * 256)
            rows = dot(from_wire, sr[at, :]).astype(BF)
            pieces.append(jnp.concatenate([rows[q * 64 : (q + 1) * 64] for q in range(4)], axis=1))
        points = jnp.concatenate(pieces, axis=0)
        update = mirror(points, mm[0], sfall[at0 : at0 + span, :], marginal)
        squares = jnp.zeros((span, 128), F32)
        for j in range(D // 128):
            piece = points[:, j * 128 : (j + 1) * 128].astype(F32)
            squares = squares + piece * piece
        inv_src = lax.rsqrt(jnp.sum(squares, axis=1, keepdims=True) + EPS)
        cosine = dot(points, tall[...], ((1,), (1,))) * inv_src * irow[0:1, :]
        weight = dot(update, ball[...], ((1,), (1,))) / R
        same = lcol[at0 : at0 + span, 0:1] == lrow[0:1, :]
        kern = jnp.where(same, weight * jnp.exp((cosine - 1.0) / TEMPER), 0.0)
        denominator = jnp.sum(kern, axis=1, keepdims=True)
        denominator = jnp.where(denominator > 0, denominator, 1.0)
        transport = (kern / denominator).astype(BF)
        image = dot(transport, tall[...]).astype(BF)
        for j in range(STEP):
            at = slice((first + j) * 256, (first + j + 1) * 256)
            isend[at, :] = dot(to_wire, quarters(image[j * 64 : (j + 1) * 64])).astype(BF)

    def group_rows(g):
        return pl.ds(16, 240) if g == 0 else pl.ds(g * 256, 256)

    for first in range(NGROUP - STEP, -1, -STEP):
        for g in range(first, first + STEP):
            remote(ss.at[group_rows(g)], sr.at[group_rows(g)], sc_s.at[g], sc_r.at[g], partner).wait_recv()
        owner_src(first)
        if first == 0:
            irecv[0:16, :] = isend[0:16, :]
        for k in order:
            g = k // GROUP
            if first <= g < first + STEP:
                at = pl.ds(k * 16, 16)
                remote(isend.at[at], irecv.at[at], rt_s.at[g], rt_r.at[g], peer(k)).start()

    mapped = jnp.zeros((ROWS, D), F32)
    for first in range(NGROUP - 4, -1, -4):
        blocks = []
        for g in range(first, first + 4):
            remote(isend.at[group_rows(g)], irecv.at[group_rows(g)], rt_s.at[g], rt_r.at[g], partner).wait_recv()
            rows = dot(from_wire, irecv[g * 256 : (g + 1) * 256, :]).astype(BF)
            blocks.append(jnp.concatenate([rows[q * 64 : (q + 1) * 64] for q in range(4)], axis=1))
        images = jnp.concatenate(blocks, axis=0)
        pick = jnp.where(iota((ROWS, 256), 1) + first * 64 == s_slot_col, 1.0, 0.0).astype(BF)
        mapped = mapped + dot(pick, images)
    mp[...] = mapped.astype(BF)

    pair.wait_send()
    remote(rest, rest, rs_s, rs_r, partner).wait_send()
    remote(rest, rest, ag_s, ag_r, partner).wait_send()
    pair_back.wait_send()
    remote(ts.at[tgt_rest], tr.at[tgt_rest], tg_s, tg_r, partner).wait_send()
    remote(ls.at[lab_rest], lr.at[lab_rest], lab_s, lab_r, partner).wait_send()
    for g in range(NGROUP):
        remote(ss.at[group_rows(g)], sr.at[group_rows(g)], sc_s.at[g], sc_r.at[g], partner).wait_send()
        remote(isend.at[group_rows(g)], irecv.at[group_rows(g)], rt_s.at[g], rt_r.at[g], partner).wait_send()


def per_device(src_points, tgt_points, src_factor, tgt_factor, inner_marginal, src_cluster, tgt_cluster):
    dma = pltpu.SemaphoreType.DMA
    vmem = pl.BlockSpec(memory_space=pltpu.VMEM)
    return pl.pallas_call(
        kernel,
        out_shape=(
            jax.ShapeDtypeStruct((ROWS, R), BF),
            jax.ShapeDtypeStruct((ROWS, R), BF),
            jax.ShapeDtypeStruct((ROWS, D), BF),
        ),
        in_specs=[vmem] * 7,
        out_specs=(vmem,) * 3,
        scratch_shapes=[
            pltpu.VMEM((2, R, D), F32),
            pltpu.VMEM((2, R, D), BF),
            pltpu.VMEM((R, D), BF),
            pltpu.VMEM((R, D), BF),
            pltpu.VMEM((64, 16, 256), BF),
            pltpu.VMEM((2, R, D), BF),
            pltpu.VMEM((NDEV * 16, 384), BF),
            pltpu.VMEM((NDEV * 16, 384), BF),
            pltpu.VMEM((NDEV * 16, 256), BF),
            pltpu.VMEM((NDEV * 16, 256), BF),
            pltpu.VMEM((NDEV, 1, NDEV), I32),
            pltpu.VMEM((NDEV, 1, NDEV), I32),
            pltpu.VMEM((SLOTS, D), BF),
            pltpu.VMEM((SLOTS, R), BF),
            pltpu.VMEM((SLOTS, R), BF),
            pltpu.VMEM((8, SLOTS), F32),
            pltpu.VMEM((SLOTS, NDEV), F32),
            pltpu.VMEM((8, SLOTS), F32),
            pltpu.VMEM((NDEV * 16, 256), BF),
            pltpu.VMEM((NDEV * 16, 256), BF),
        ]
        + [dma] * 12
        + [dma((NGROUP,))] * 4,
        compiler_params=pltpu.CompilerParams(collective_id=0, has_side_effects=True, vmem_limit_bytes=60 << 20),
        name="transport",
    )(
        src_points,
        tgt_points,
        src_factor,
        tgt_factor,
        inner_marginal.reshape(1, R),
        src_cluster.reshape(1, ROWS),
        tgt_cluster.reshape(1, ROWS),
    )


def solution(mesh):
    both = P(("src", "tgt"), None)
    flat = P(("src", "tgt"))
    return jax.shard_map(
        per_device,
        mesh=mesh,
        in_specs=(both, both, both, both, P(), flat, flat),
        out_specs=(both, both, both),
        check_vma=False,
    )
```

time: 230 us -> 96.2 us (0.42)
  Pallas kernels: 0 us -> 91.4 us
  blocking collectives: 77.9 us -> 0 us
  waiting for transfers between devices: 72.3 us -> 0 us
  starting transfers between devices: 40.3 us -> 0 us
  local copies, waits for them, and re-layouts: 24.9 us -> 3.99 us
  matrix products: 8.35 us -> 0 us
  other arithmetic: 4.6 us -> 0 us
    pallas_call x0 -> x1, Pallas kernels: none -> 91.4 us  [per_device(): pl.pallas_call(kernel, out_shape=(jax.ShapeDtypeStruct((ROWS, R), BF), ja...]
    psum x1 -> x0, blocking collectives: 77.9 us -> none  [per_device(): tgt_total, src_total = lax.psum((tgt_part, src_part), ('src', 'tgt'))]
    all_to_all x7 -> x0, waiting for transfers between devices: 72.3 us -> none  [the longest x1 19.1 us: per_device(): lax.all_to_all(images, ('src', 'tgt'), split_axis=0, concat_axis=0, tiled...]
    all_to_all x7 -> x0, starting transfers between devices: 40.3 us -> none  [the longest x1 11.5 us: per_device(): lax.all_to_all(tgt_labels, ('src', 'tgt'), split_axis=0, concat_axis=0, t...]
    all_to_all x13 -> x0, local copies, waits for them, and re-layouts: 10.6 us -> none  [the longest x2 2.41 us: per_device(): lax.all_to_all(src_rows, ('src', 'tgt'), split_axis=0, concat_axis=0, til...]
    scatter x6 -> x0, local copies, waits for them, and re-layouts: 9.85 us -> none  [the longest x2 3.82 us: pack_rows(): jnp.zeros((buffer_len, points.shape[1]), jnp.bfloat16).at[slot_index]]
    dot_general x9 -> x0, matrix products: 8.35 us -> none  [the longest x1 2.19 us: one_block(): lax.dot_general(rows_block, tgt_rows, (((1,), (1,)), ((), ())), preferred...]
  transfers between devices with their start and end apart: 7 -> 0, of which waited for: 6 -> 0; matrix products, arithmetic and copies ran while one was open for 8% -> 0% of each run, Pallas kernels for 0% -> 0%
where the time goes in v1:
time: 96.2 us; the launch traced here: 96 us
  Pallas kernels  91.4 us (95%)
  local copies, waits for them, and re-layouts  3.99 us (4%)
    pallas_call x1, Pallas kernels, per_device(): pl.pallas_call(kernel, out_shape=(jax.ShapeDtypeStruct((ROWS, R), BF), ja...  91.4 us
    unnamed x5, local copies, waits for them, and re-layouts  3.99 us

profile of v1, /device:TPU:1, one launch (start us, length us, event | category | flops | bytes accessed | tf_op | source)
XLA Modules:
  0.0 96.0 jit_solution(16309353234925356642)
XLA Ops:
  0.6 91.4 %transport.1 = (bf16[256,256]{1,0:T(8,128)(2,1)}, bf16[256,256]{1,0:T(8,128)(2,1)}, bf16[256,1024]{1,0:T(8,128)(2,1)}) custom-call(bf16[256,1024]{1,0:T(8,128)(2,1)} %sp.1, bf16[256,1024]{1,0:T(8,128)(2,1)} %tp.1, bf16[256,256]{1,0:T(8,128)(2,1)} %sf.1, bf16[256,256]{1,0:T(8,128)(2,1)} %tf.1, f32[1,256]{1,0:T(1,128)} %bitcast.3, s32[1,256]{1,0:T(1,128)} %bitcast.4, ...), custom_call_target="tpu_custom_call" | custom-call | tf_op jit(solution)/shard_map/transport/pallas_call | solution.py:339
  92.0 0.0 copy-start
  92.0 1.6 %copy.13 = bf16[256,256]{1,0:T(8,128)(2,1)} copy(bf16[256,256]{1,0:T(8,128)(2,1)} %get-tuple-element.6) | data formatting | bytes 262144
  93.6 1.6 %copy.14 = bf16[256,256]{1,0:T(8,128)(2,1)} copy(bf16[256,256]{1,0:T(8,128)(2,1)} %get-tuple-element.7) | data formatting | bytes 262144
  95.2 0.0 copy-done
  95.2 0.8 copy.15
Async XLA Ops:
  92.0 3.2 %copy-start = (bf16[256,1024]{1,0:T(8,128)(2,1)S(1)}, bf16[256,1024]{1,0:T(8,128)(2,1)}, u32[]{:S(2)}) copy-start(bf16[256,1024]{1,0:T(8,128)(2,1)} %get-tuple-element.8) | copy-start | bytes 1572868

commit v2 on v1

v2 whole, which is shorter than its diff:
```python
import jax
import jax.numpy as jnp
from jax import lax
from jax.experimental import pallas as pl
from jax.experimental.pallas import tpu as pltpu
from jax.sharding import PartitionSpec as P

CL_DEV = 2
CAP = 4
GAMMA = 2.0
TEMPER = 0.03
EPS = 1e-06

D = 1024
R = 256
ROWS = 256
NDEV = 128
SLOTS = NDEV * CAP
QUART = D // 4
GROUP = 16
NGROUP = NDEV // GROUP
GROUPS = tuple(range(NGROUP - 1, -1, -1))
PACK_EARLY = 2
SENT_FIRST = 2
PACK_PAIR = 4
SENT_SECOND = 5
STEP = 2
LAST = 2
VLIM = 56 << 20
MESH = pl.DeviceIdType.MESH
BF = jnp.bfloat16
F32 = jnp.float32
I32 = jnp.int32


def offset_of(k):
    x1, y1, z1, x0, y0, z0, c = ((k >> b) & 1 for b in (6, 5, 4, 3, 2, 1, 0))
    return (y1 * 8 + y0 * 4 + x1 * 2 + x0, z1 * 4 + z0 * 2 + c)


def hops(k):
    ds, dt = offset_of(k)
    ring = (0, 1, 2, 1)
    return ring[ds // 4] + ring[ds % 4] + ring[dt // 2]


def place_of(owner):
    bit = lambda b: (owner // (1 << b)) % 2
    y1, y0, x1, x0, z1, z0, c = (bit(b) for b in (6, 5, 4, 3, 2, 1, 0))
    return x1 * 64 + y1 * 32 + z1 * 16 + x0 * 8 + y0 * 4 + z0 * 2 + c


def flips(value, bits):
    parts = [(value // (1 << b)) % 2 for b in range(bits)]
    out = []
    for m in range(1 << bits):
        total = 0
        for b in range(bits):
            total = total + ((1 - parts[b]) if (m >> b) & 1 else parts[b]) * (1 << b)
        out.append(total)
    return out


def dot(a, b, dims=((1,), (0,)), precision=None):
    return lax.dot_general(a, b, (dims, ((), ())), preferred_element_type=F32, precision=precision)


def iota(shape, axis):
    return lax.broadcasted_iota(I32, shape, axis)


def mirror(points, total_t, factor, marginal):
    gradient = dot(points, total_t, ((1,), (1,))) / marginal
    row_scale = jnp.max(jnp.abs(gradient), axis=1, keepdims=True) + EPS
    tilted = factor.astype(F32) * jnp.exp(GAMMA * gradient / row_scale)
    mean = jnp.mean(tilted, axis=1, keepdims=True)
    return (tilted / jnp.where(mean > 0, mean, 1.0)).astype(BF)


def slots_of(cluster_row, me_bits):
    eye = iota((ROWS, ROWS), 0) == iota((ROWS, ROWS), 1)
    owner_row = cluster_row // CL_DEV
    cluster_col = jnp.sum(jnp.where(eye, cluster_row, 0).astype(F32), axis=1, keepdims=True).astype(I32)
    owner_col = cluster_col // CL_DEV
    same = owner_col == owner_row
    below = iota((ROWS, ROWS), 0) < iota((ROWS, ROWS), 1)
    above = iota((ROWS, ROWS), 1) < iota((ROWS, ROWS), 0)
    rank_row = jnp.sum(jnp.where(same & below, 1.0, 0.0), axis=0, keepdims=True).astype(I32)
    rank_col = jnp.sum(jnp.where(same & above, 1.0, 0.0), axis=1, keepdims=True).astype(I32)

    def block(owner):
        place = place_of(owner)
        total = 0
        for b in range(7):
            mine = me_bits[b]
            theirs = (place // (1 << b)) % 2
            total = total + (mine + theirs - 2 * mine * theirs) * (1 << b)
        return total

    return block(owner_row), rank_row, block(owner_col), rank_col, cluster_col


def kernel(
    sp_in, tp_in, sf_in, tf_in, marg, scl, tcl,
    su, tu, mp,
    sp, tp, sf, tf, pf, pp, rx, cs, rr, mm, ts, tr, ss, sr, ls, lr, tall, ball, sfall, tfall, isend, irecv,
    in_sem, pair_s, pair_r, rs_s, rs_r, ag_s, ag_r, pb_s, pb_r, tg_s, tg_r, sc_s, sc_r, rt_s, rt_r, lab_s, lab_r,
):
    s = lax.axis_index("src")
    t = lax.axis_index("tgt")
    z = t // 2
    core = t % 2
    sx = flips(s, 4)
    tx = flips(t, 3)
    zx = flips(z, 2)

    def peer(k):
        ds, dt = offset_of(k)
        return (sx[ds], tx[dt])

    partner = (s, tx[1])

    loads = [
        pltpu.make_async_copy(src, dst, in_sem.at[j])
        for j, (src, dst) in enumerate(((tp_in, tp), (tf_in, tf), (sp_in, sp), (sf_in, sf)))
    ]
    for load in loads:
        load.start()

    barrier = pltpu.get_barrier_semaphore()
    for k in sorted(range(1, NDEV), key=lambda k: -hops(k)):
        pl.semaphore_signal(barrier, inc=1, device_id=peer(k), device_id_type=MESH)

    def remote(src, dst, send, recv, device):
        return pltpu.make_async_remote_copy(
            src_ref=src, dst_ref=dst, send_sem=send, recv_sem=recv, device_id=device, device_id_type=MESH
        )

    def group_rows(g):
        return pl.ds(16, 240) if g == 0 else pl.ds(g * 256, 256)

    def group_blocks(g):
        return pl.ds(1, 15) if g == 0 else pl.ds(g * 16, 16)

    orders = [sorted((k for k in range(g * GROUP, (g + 1) * GROUP) if k), key=lambda k: -hops(k)) for g in range(NGROUP)]

    me = s * 8 + t
    my_place = place_of(me)
    me_bits = [(my_place // (1 << b)) % 2 for b in range(7)]
    s_blk_row, s_rank_row, s_blk_col, s_rank_col, s_cl_col = slots_of(scl[...], me_bits)
    t_blk_row, t_rank_row, t_blk_col, t_rank_col, t_cl_col = slots_of(tcl[...], me_bits)
    s_slot_row = s_blk_row * CAP + s_rank_row
    t_slot_row = t_blk_row * CAP + t_rank_row
    s_slot_col = s_blk_col * CAP + s_rank_col

    lane = iota((ROWS, NDEV), 1)
    blk = iota((NDEV, ROWS), 0)
    s_val = jnp.where(lane == s_rank_col, (s_cl_col % CL_DEV + 1).astype(F32), 0.0).astype(BF)
    t_val = jnp.where(lane == t_rank_col + CAP, (t_cl_col % CL_DEV + 1).astype(F32), 0.0).astype(BF)
    s_hot = jnp.where(blk == s_blk_row, 1.0, 0.0).astype(BF)
    t_hot = jnp.where(blk == t_blk_row, 1.0, 0.0).astype(BF)
    labels = (dot(s_hot, s_val) + dot(t_hot, t_val)).astype(I32)
    ls[...] = labels.reshape(NDEV, 1, NDEV)
    lr[0] = ls[0]

    loads[0].wait()
    loads[1].wait()
    part = dot(tf[...], tp[...], ((0,), (0,)))
    pf[0] = part
    pp[0] = part.astype(BF)
    loads[2].wait()
    loads[3].wait()
    part = dot(sf[...], sp[...], ((0,), (0,)))
    pf[1] = part
    pp[1] = part.astype(BF)

    row = iota((ROWS, ROWS), 0)
    col = iota((ROWS, ROWS), 1)
    to_wire = jnp.where(col == (row // 4 % 4) * 64 + (row // 16) * 4 + row % 4, 1.0, 0.0).astype(BF)
    from_wire = jnp.where(row == (col // 4 % 4) * 64 + (col // 16) * 4 + col % 4, 1.0, 0.0).astype(BF)

    def hot_rows(g, slot_row):
        return jnp.where(iota((64, ROWS), 0) + g * 64 == slot_row, 1.0, 0.0).astype(BF)

    def quarters(x):
        return jnp.concatenate([x[:, q * QUART : (q + 1) * QUART] for q in range(4)], axis=0)

    def rows_of(x):
        return jnp.concatenate([x[q * 64 : (q + 1) * 64] for q in range(4)], axis=1)

    def pack_tgt(g):
        t_sel = hot_rows(g, t_slot_row)
        s_sel = hot_rows(g, s_slot_row)
        rows = dot(t_sel, tp[...]).astype(BF)
        f_t = dot(t_sel, tf[...]).astype(BF)
        f_s = dot(s_sel, sf[...]).astype(BF)
        facs = jnp.concatenate([f_s[:, :128], f_s[:, 128:], f_t[:, :128], f_t[:, 128:]], axis=0)
        at = slice(g * 256, (g + 1) * 256)
        ts[at, 0:QUART] = dot(to_wire, quarters(rows)).astype(BF)
        ts[at, QUART : QUART + 128] = dot(to_wire, facs).astype(BF)
        if g == 0:
            tr[0:16, :] = ts[0:16, :]

    def pack_src(g):
        rows = dot(hot_rows(g, s_slot_row), sp[...]).astype(BF)
        ss[g * 256 : (g + 1) * 256, :] = dot(to_wire, quarters(rows)).astype(BF)
        if g == 0:
            sr[0:16, :] = ss[0:16, :]

    def send_tgt(g):
        for k in orders[g]:
            at = pl.ds(k * 16, 16)
            remote(ts.at[at], tr.at[at], tg_s.at[g], tg_r.at[g], peer(k)).start()
            remote(ls.at[k], lr.at[k], lab_s.at[g], lab_r.at[g], peer(k)).start()

    def send_src(g):
        for k in orders[g]:
            at = pl.ds(k * 16, 16)
            remote(ss.at[at], sr.at[at], sc_s.at[g], sc_r.at[g], peer(k)).start()

    for g in GROUPS[:PACK_EARLY]:
        pack_tgt(g)

    pl.semaphore_wait(barrier, NDEV - 1)

    pair = remote(pp.at[1 - core], rx, pair_s, pair_r, partner)
    pair.start()

    for g in GROUPS[:SENT_FIRST]:
        send_tgt(g)
    for g in GROUPS[PACK_EARLY:PACK_PAIR]:
        pack_tgt(g)

    pair.wait_recv()
    cs[...] = (pf[core] + rx[...].astype(F32)).astype(BF)

    for kc in range(1, 64):
        ds, dz = kc // 4, kc % 4
        remote(
            cs.at[pl.ds(pl.multiple_of(sx[ds] * 16, 16), 16), pl.ds(pl.multiple_of(zx[dz] * 256, 256), 256)],
            rr.at[kc], rs_s, rs_r, (sx[ds], tx[dz * 2]),
        ).start()

    for g in GROUPS[SENT_FIRST:PACK_PAIR]:
        send_tgt(g)
    for i in range(PACK_PAIR, NGROUP):
        pack_tgt(GROUPS[i])
        if i < SENT_SECOND:
            send_tgt(GROUPS[i])
    for g in GROUPS:
        pack_src(g)

    rest = rr.at[pl.ds(1, 63)]
    remote(rest, rest, rs_s, rs_r, partner).wait_recv()
    my_rows = pl.ds(pl.multiple_of(s * 16, 16), 16)
    my_cols = pl.ds(pl.multiple_of(z * 256, 256), 256)
    total = cs[my_rows, my_cols].astype(F32)
    for kc in range(1, 64):
        total = total + rr[kc].astype(F32)
    mm[core, my_rows, my_cols] = total.astype(BF)

    mine = mm.at[core, my_rows, my_cols]
    for kc in range(1, 64):
        ds, dz = kc // 4, kc % 4
        remote(mine, mine, ag_s, ag_r, (sx[ds], tx[dz * 2])).start()
    for g in GROUPS[SENT_SECOND:]:
        send_tgt(g)
    for g in GROUPS:
        send_src(g)

    def owner_tgt(g):
        at = slice(g * 256, (g + 1) * 256)
        to = slice(g * 64, (g + 1) * 64)
        remote(ts.at[group_rows(g)], tr.at[group_rows(g)], tg_s.at[g], tg_r.at[g], partner).wait_recv()
        remote(ls.at[group_blocks(g)], lr.at[group_blocks(g)], lab_s.at[g], lab_r.at[g], partner).wait_recv()
        tall[to, :] = rows_of(dot(from_wire, tr[at, 0:QUART]).astype(BF))
        facs = dot(from_wire, tr[at, QUART : QUART + 128]).astype(BF)
        sfall[to, :] = jnp.concatenate([facs[0:64], facs[64:128]], axis=1)
        tfall[to, :] = jnp.concatenate([facs[128:192], facs[192:256]], axis=1)

    for g in GROUPS[:SENT_SECOND]:
        owner_tgt(g)

    remote(rest, rest, ag_s, ag_r, partner).wait_recv()
    pair_back = remote(mm.at[core], mm.at[core], pb_s, pb_r, partner)
    pair_back.start()

    for g in GROUPS[SENT_SECOND:]:
        owner_tgt(g)

    def squares_of(points):
        total = jnp.zeros((points.shape[0], 128), F32)
        for j in range(D // 128):
            piece = points[:, j * 128 : (j + 1) * 128].astype(F32)
            total = total + piece * piece
        return total

    sums = dot(jnp.ones((8, 128), F32), squares_of(tall[...]), ((1,), (1,)), precision=lax.Precision.HIGHEST)
    inv_tgt = lax.rsqrt(sums + EPS)[0:1, :]

    got = lr[...].reshape(NDEV, NDEV).astype(F32).astype(BF)
    spread = jnp.where(iota((SLOTS, NDEV), 0) // CAP == iota((SLOTS, NDEV), 1), 1.0, 0.0).astype(BF)
    per_slot = dot(spread, got)
    slot_lane = iota((SLOTS, NDEV), 1) - iota((SLOTS, NDEV), 0) % CAP
    src_lab = jnp.sum(jnp.where(slot_lane == 0, per_slot, 0.0), axis=1, keepdims=True)
    tgt_lab = jnp.where(slot_lane == CAP, per_slot, 0.0).astype(BF)
    tgt_lab = dot(jnp.ones((8, NDEV), BF), tgt_lab, ((1,), (1,)))[0:1, :]

    remote(mm.at[1 - core], mm.at[1 - core], pb_s, pb_r, partner).wait_recv()
    marginal = marg[...]
    ball[...] = mirror(tall[...], mm[1], tfall[...], marginal)

    span = 64 * STEP

    def owner_src(groups):
        lo = min(groups)
        at0 = lo * 64
        pieces = [rows_of(dot(from_wire, sr[g * 256 : (g + 1) * 256, :]).astype(BF)) for g in sorted(groups)]
        points = jnp.concatenate(pieces, axis=0)
        update = mirror(points, mm[0], sfall[at0 : at0 + span, :], marginal)
        inv_src = lax.rsqrt(jnp.sum(squares_of(points), axis=1, keepdims=True) + EPS)
        cosine = dot(points, tall[...], ((1,), (1,))) * inv_src * inv_tgt
        weight = dot(update, ball[...], ((1,), (1,))) / R
        same = src_lab[at0 : at0 + span] == tgt_lab
        kern = jnp.where(same, weight * jnp.exp((cosine - 1.0) / TEMPER), 0.0)
        denominator = jnp.sum(kern, axis=1, keepdims=True)
        denominator = jnp.where(denominator > 0, denominator, 1.0)
        transport = (kern / denominator).astype(BF)
        image = dot(transport, tall[...]).astype(BF)
        for j, g in enumerate(sorted(groups)):
            isend[g * 256 : (g + 1) * 256, :] = dot(to_wire, quarters(image[j * 64 : (j + 1) * 64])).astype(BF)

    for first in range(0, NGROUP, STEP):
        groups = GROUPS[first : first + STEP]
        for g in groups:
            remote(ss.at[group_rows(g)], sr.at[group_rows(g)], sc_s.at[g], sc_r.at[g], partner).wait_recv()
        owner_src(groups)
        if 0 in groups:
            irecv[0:16, :] = isend[0:16, :]
        for g in groups:
            for k in orders[g]:
                at = pl.ds(k * 16, 16)
                remote(isend.at[at], irecv.at[at], rt_s.at[g], rt_r.at[g], peer(k)).start()

    su[...] = mirror(sp[...], mm[0], sf[...], marginal)
    tu[...] = mirror(tp[...], mm[1], tf[...], marginal)

    mapped = jnp.zeros((ROWS, D), F32)
    for first in range(0, NGROUP, LAST):
        groups = sorted(GROUPS[first : first + LAST])
        blocks = []
        for g in groups:
            remote(isend.at[group_rows(g)], irecv.at[group_rows(g)], rt_s.at[g], rt_r.at[g], partner).wait_recv()
            blocks.append(rows_of(dot(from_wire, irecv[g * 256 : (g + 1) * 256, :]).astype(BF)))
        images = jnp.concatenate(blocks, axis=0)
        pick = jnp.where(iota((ROWS, 64 * LAST), 1) + groups[0] * 64 == s_slot_col, 1.0, 0.0).astype(BF)
        mapped = mapped + dot(pick, images)
    mp[...] = mapped.astype(BF)

    pair.wait_send()
    remote(rest, rest, rs_s, rs_r, partner).wait_send()
    remote(rest, rest, ag_s, ag_r, partner).wait_send()
    pair_back.wait_send()
    for g in range(NGROUP):
        remote(ts.at[group_rows(g)], tr.at[group_rows(g)], tg_s.at[g], tg_r.at[g], partner).wait_send()
        remote(ls.at[group_blocks(g)], lr.at[group_blocks(g)], lab_s.at[g], lab_r.at[g], partner).wait_send()
        remote(ss.at[group_rows(g)], sr.at[group_rows(g)], sc_s.at[g], sc_r.at[g], partner).wait_send()
        remote(isend.at[group_rows(g)], irecv.at[group_rows(g)], rt_s.at[g], rt_r.at[g], partner).wait_send()


def per_device(src_points, tgt_points, src_factor, tgt_factor, inner_marginal, src_cluster, tgt_cluster):
    dma = pltpu.SemaphoreType.DMA
    vmem = pl.BlockSpec(memory_space=pltpu.VMEM)
    hbm = pl.BlockSpec(memory_space=pl.ANY)
    return pl.pallas_call(
        kernel,
        out_shape=(
            pltpu.VMEM((ROWS, R), BF),
            pltpu.VMEM((ROWS, R), BF),
            pltpu.VMEM((ROWS, D), BF),
        ),
        in_specs=[hbm] * 4 + [vmem] * 3,
        out_specs=(vmem,) * 3,
        scratch_shapes=[
            pltpu.VMEM((ROWS, D), BF),
            pltpu.VMEM((ROWS, D), BF),
            pltpu.VMEM((ROWS, R), BF),
            pltpu.VMEM((ROWS, R), BF),
            pltpu.VMEM((2, R, D), F32),
            pltpu.VMEM((2, R, D), BF),
            pltpu.VMEM((R, D), BF),
            pltpu.VMEM((R, D), BF),
            pltpu.VMEM((64, 16, 256), BF),
            pltpu.VMEM((2, R, D), BF),
            pltpu.VMEM((NDEV * 16, 384), BF),
            pltpu.VMEM((NDEV * 16, 384), BF),
            pltpu.VMEM((NDEV * 16, 256), BF),
            pltpu.VMEM((NDEV * 16, 256), BF),
            pltpu.VMEM((NDEV, 1, NDEV), I32),
            pltpu.VMEM((NDEV, 1, NDEV), I32),
            pltpu.VMEM((SLOTS, D), BF),
            pltpu.VMEM((SLOTS, R), BF),
            pltpu.VMEM((SLOTS, R), BF),
            pltpu.VMEM((SLOTS, R), BF),
            pltpu.VMEM((NDEV * 16, 256), BF),
            pltpu.VMEM((NDEV * 16, 256), BF),
        ]
        + [dma((4,))]
        + [dma] * 8
        + [dma((NGROUP,))] * 8,
        compiler_params=pltpu.CompilerParams(collective_id=0, has_side_effects=True, vmem_limit_bytes=VLIM),
        name="transport",
    )(
        src_points,
        tgt_points,
        src_factor,
        tgt_factor,
        inner_marginal.reshape(1, R),
        src_cluster.reshape(1, ROWS),
        tgt_cluster.reshape(1, ROWS),
    )


def solution(mesh):
    both = P(("src", "tgt"), None)
    flat = P(("src", "tgt"))
    return jax.shard_map(
        per_device,
        mesh=mesh,
        in_specs=(both, both, both, both, P(), flat, flat),
        out_specs=(both, both, both),
        check_vma=False,
    )
```

time: 96.2 us -> 81.3 us (0.85)
  Pallas kernels: 91.4 us -> 78.4 us
  local copies, waits for them, and re-layouts: 3.99 us -> 2.11 us
    pallas_call x1, Pallas kernels: 91.4 us -> 78.4 us  [per_device(): pl.pallas_call(kernel, out_shape=(pltpu.VMEM((ROWS, R), BF), pltpu.VMEM((...]
    unnamed x5 -> x3, local copies, waits for them, and re-layouts: 3.99 us -> 2.11 us
where the time goes in v2:
time: 81.3 us; the launch traced here: 81.2 us
  Pallas kernels  78.4 us (96%)
  local copies, waits for them, and re-layouts  2.11 us (3%)
    pallas_call x1, Pallas kernels, per_device(): pl.pallas_call(kernel, out_shape=(pltpu.VMEM((ROWS, R), BF), pltpu.VMEM((...  78.4 us
    unnamed x3, local copies, waits for them, and re-layouts  2.11 us

profile of v2, /device:TPU:1, one launch (start us, length us, event | category | flops | bytes accessed | tf_op | source)
XLA Modules:
  0.0 81.2 jit_solution(10123220712677967965)
XLA Ops:
  0.6 78.4 %transport.1 = (bf16[256,256]{1,0:T(8,128)(2,1)S(1)}, bf16[256,256]{1,0:T(8,128)(2,1)S(1)}, bf16[256,1024]{1,0:T(8,128)(2,1)S(1)}) custom-call(bf16[256,1024]{1,0:T(8,128)(2,1)} %sp_in.1, bf16[256,1024]{1,0:T(8,128)(2,1)} %tp_in.1, bf16[256,256]{1,0:T(8,128)(2,1)} %sf_in.1, bf16[256,256]{1,0:T(8,128)(2,1)} %tf_in.1, f32[1,256]{1,0:T(1,128)} %bitcast.3, ...), custom_call_target="tpu_custom_call" | custom-call | tf_op jit(solution)/shard_map/transport/pallas_call | solution.py:375
  79.1 0.7 copy.13
  79.7 0.7 copy.14
  80.4 0.8 copy.15

commit v3 on v2

--- a/solution.py
+++ b/solution.py
@@ -19,11 +19,12 @@
 QUART = D // 4
 GROUP = 16
 NGROUP = NDEV // GROUP
-GROUPS = tuple(range(NGROUP - 1, -1, -1))
+GROUPS = (5, 4, 7, 6, 3, 2, 1, 0)
 PACK_EARLY = 2
 SENT_FIRST = 2
 PACK_PAIR = 4
-SENT_SECOND = 5
+SENT_SECOND = 8
+SRC_EARLY = 0
 STEP = 2
 LAST = 2
 VLIM = 56 << 20
@@ -34,7 +35,8 @@
 
 
 def offset_of(k):
-    x1, y1, z1, x0, y0, z0, c = ((k >> b) & 1 for b in (6, 5, 4, 3, 2, 1, 0))
+    g2, g1, g0, x1, x0, y1, y0 = ((k >> b) & 1 for b in (6, 5, 4, 3, 2, 1, 0))
+    z1, z0, c = g2 ^ x1 ^ y1, g1 ^ x0 ^ y0, g0 ^ x0 ^ y1
     return (y1 * 8 + y0 * 4 + x1 * 2 + x0, z1 * 4 + z0 * 2 + c)
 
 
@@ -47,7 +49,8 @@
 def place_of(owner):
     bit = lambda b: (owner // (1 << b)) % 2
     y1, y0, x1, x0, z1, z0, c = (bit(b) for b in (6, 5, 4, 3, 2, 1, 0))
-    return x1 * 64 + y1 * 32 + z1 * 16 + x0 * 8 + y0 * 4 + z0 * 2 + c
+    g2, g1, g0 = (z1 + x1 + y1) % 2, (z0 + x0 + y0) % 2, (c + x0 + y1) % 2
+    return g2 * 64 + g1 * 32 + g0 * 16 + x1 * 8 + x0 * 4 + y1 * 2 + y0
 
 
 def flips(value, bits):
@@ -119,6 +122,7 @@
         return (sx[ds], tx[dt])
 
     partner = (s, tx[1])
+    chips = sorted(range(1, 64), key=lambda k: ((k // 16) ^ (k // 4 % 4) ^ (k % 4), k % 4))
 
     loads = [
         pltpu.make_async_copy(src, dst, in_sem.at[j])
@@ -234,7 +238,7 @@
     pair.wait_recv()
     cs[...] = (pf[core] + rx[...].astype(F32)).astype(BF)
 
-    for kc in range(1, 64):
+    for kc in chips:
         ds, dz = kc // 4, kc % 4
         remote(
             cs.at[pl.ds(pl.multiple_of(sx[ds] * 16, 16), 16), pl.ds(pl.multiple_of(zx[dz] * 256, 256), 256)],
@@ -247,8 +251,10 @@
         pack_tgt(GROUPS[i])
         if i < SENT_SECOND:
             send_tgt(GROUPS[i])
-    for g in GROUPS:
+    for i, g in enumerate(GROUPS):
         pack_src(g)
+        if i < SRC_EARLY:
+            send_src(g)
 
     rest = rr.at[pl.ds(1, 63)]
     remote(rest, rest, rs_s, rs_r, partner).wait_recv()
@@ -260,12 +266,12 @@
     mm[core, my_rows, my_cols] = total.astype(BF)
 
     mine = mm.at[core, my_rows, my_cols]
-    for kc in range(1, 64):
+    for kc in chips:
         ds, dz = kc // 4, kc % 4
         remote(mine, mine, ag_s, ag_r, (sx[ds], tx[dz * 2])).start()
     for g in GROUPS[SENT_SECOND:]:
         send_tgt(g)
-    for g in GROUPS:
+    for g in GROUPS[SRC_EARLY:]:
         send_src(g)
 
     def owner_tgt(g):
@@ -368,11 +374,22 @@
         remote(isend.at[group_rows(g)], irecv.at[group_rows(g)], rt_s.at[g], rt_r.at[g], partner).wait_send()
 
 
+def put_out(su, tu, mp, su_out, tu_out, mp_out, sems):
+    copies = [
+        pltpu.make_async_copy(src, dst, sems.at[j])
+        for j, (src, dst) in enumerate(((mp, mp_out), (su, su_out), (tu, tu_out)))
+    ]
+    for copy in copies:
+        copy.start()
+    for copy in copies:
+        copy.wait()
+
+
 def per_device(src_points, tgt_points, src_factor, tgt_factor, inner_marginal, src_cluster, tgt_cluster):
     dma = pltpu.SemaphoreType.DMA
     vmem = pl.BlockSpec(memory_space=pltpu.VMEM)
     hbm = pl.BlockSpec(memory_space=pl.ANY)
-    return pl.pallas_call(
+    su, tu, mp = pl.pallas_call(
         kernel,
         out_shape=(
             pltpu.VMEM((ROWS, R), BF),
@@ -419,6 +436,15 @@
         src_cluster.reshape(1, ROWS),
         tgt_cluster.reshape(1, ROWS),
     )
+    shape = jax.ShapeDtypeStruct
+    return pl.pallas_call(
+        put_out,
+        out_shape=(shape((ROWS, R), BF), shape((ROWS, R), BF), shape((ROWS, D), BF)),
+        in_specs=[vmem] * 3,
+        out_specs=(hbm,) * 3,
+        scratch_shapes=[dma((3,))],
+        name="put_out",
+    )(*(pltpu.with_memory_space_constraint(x, pltpu.VMEM) for x in (su, tu, mp)))
 
 
 def solution(mesh):

time: 81.3 us -> 72.1 us (0.89)
  Pallas kernels: 78.4 us -> 70.9 us
  local copies, waits for them, and re-layouts: 2.11 us -> 0 us
    pallas_call x1, Pallas kernels: 78.4 us -> 70 us  [per_device(): pl.pallas_call(kernel, out_shape=(pltpu.VMEM((ROWS, R), BF), pltpu.VMEM((...]
    unnamed x3 -> x0, local copies, waits for them, and re-layouts: 2.11 us -> none
    pallas_call x0 -> x1, Pallas kernels: none -> 0.9 us  [per_device(): pl.pallas_call(put_out, out_shape=(shape((ROWS, R), BF), shape((ROWS, R),...]
where the time goes in v3:
time: 72.1 us; the launch traced here: 71.7 us
  Pallas kernels  70.9 us (98%)
  between operations  0.8 us (1%)
    pallas_call x1, Pallas kernels, per_device(): pl.pallas_call(kernel, out_shape=(pltpu.VMEM((ROWS, R), BF), pltpu.VMEM((...  70 us

profile of v3, /device:TPU:1, one launch (start us, length us, event | category | flops | bytes accessed | tf_op | source)
XLA Modules:
  0.0 71.7 jit_solution(3780316993609387922)
XLA Ops:
  0.6 70.0 %transport.1 = (bf16[256,256]{1,0:T(8,128)(2,1)S(1)}, bf16[256,256]{1,0:T(8,128)(2,1)S(1)}, bf16[256,1024]{1,0:T(8,128)(2,1)S(1)}) custom-call(bf16[256,1024]{1,0:T(8,128)(2,1)} %sp_in.1, bf16[256,1024]{1,0:T(8,128)(2,1)} %tp_in.1, bf16[256,256]{1,0:T(8,128)(2,1)} %sf_in.1, bf16[256,256]{1,0:T(8,128)(2,1)} %tf_in.1, f32[1,256]{1,0:T(1,128)} %bitcast.3, ...), custom_call_target="tpu_custom_call" | custom-call | tf_op jit(solution)/shard_map/transport/pallas_call | solution.py:392
  70.6 0.9 %put_out.1 = (bf16[256,256]{1,0:T(8,128)(2,1)}, bf16[256,256]{1,0:T(8,128)(2,1)}, bf16[256,1024]{1,0:T(8,128)(2,1)}) custom-call(bf16[256,256]{1,0:T(8,128)(2,1)S(1)} %get-tuple-element.6.su, bf16[256,256]{1,0:T(8,128)(2,1)S(1)} %get-tuple-element.7.tu, bf16[256,1024]{1,0:T(8,128)(2,1)S(1)} %get-tuple-element.8.mp), custom_call_target="tpu_custom_call" | custom-call | tf_op jit(solution)/shard_map/put_out/pallas_call | solution.py:440

commit v4 on v3

--- a/solution.py
+++ b/solution.py
@@ -122,7 +122,7 @@
         return (sx[ds], tx[dt])
 
     partner = (s, tx[1])
-    chips = sorted(range(1, 64), key=lambda k: ((k // 16) ^ (k // 4 % 4) ^ (k % 4), k % 4))
+    chips = sorted(range(1, 64), key=lambda k: -((0, 1, 2, 1)[k // 16] + (0, 1, 2, 1)[k // 4 % 4] + (0, 1, 2, 1)[k % 4]))
 
     loads = [
         pltpu.make_async_copy(src, dst, in_sem.at[j])

time: 72.1 us -> 71.9 us (level)
  no operation moved by 1% of the time
where the time goes in v4:
time: 71.9 us; the launch traced here: 71.8 us
  Pallas kernels  71 us (99%)
  between operations  0.8 us (1%)
    pallas_call x1, Pallas kernels, per_device(): pl.pallas_call(kernel, out_shape=(pltpu.VMEM((ROWS, R), BF), pltpu.VMEM((...  70.1 us

profile of v4, /device:TPU:1, one launch (start us, length us, event | category | flops | bytes accessed | tf_op | source)
XLA Modules:
  0.0 71.8 jit_solution(193984944343907104)
XLA Ops:
  0.6 70.1 %transport.1 = (bf16[256,256]{1,0:T(8,128)(2,1)S(1)}, bf16[256,256]{1,0:T(8,128)(2,1)S(1)}, bf16[256,1024]{1,0:T(8,128)(2,1)S(1)}) custom-call(bf16[256,1024]{1,0:T(8,128)(2,1)} %sp_in.1, bf16[256,1024]{1,0:T(8,128)(2,1)} %tp_in.1, bf16[256,256]{1,0:T(8,128)(2,1)} %sf_in.1, bf16[256,256]{1,0:T(8,128)(2,1)} %tf_in.1, f32[1,256]{1,0:T(1,128)} %bitcast.3, ...), custom_call_target="tpu_custom_call" | custom-call | tf_op jit(solution)/shard_map/transport/pallas_call | solution.py:392
  70.7 0.9 %put_out.1 = (bf16[256,256]{1,0:T(8,128)(2,1)}, bf16[256,256]{1,0:T(8,128)(2,1)}, bf16[256,1024]{1,0:T(8,128)(2,1)}) custom-call(bf16[256,256]{1,0:T(8,128)(2,1)S(1)} %get-tuple-element.6.su, bf16[256,256]{1,0:T(8,128)(2,1)S(1)} %get-tuple-element.7.tu, bf16[256,1024]{1,0:T(8,128)(2,1)S(1)} %get-tuple-element.8.mp), custom_call_target="tpu_custom_call" | custom-call | tf_op jit(solution)/shard_map/put_out/pallas_call | solution.py:440

commit v5 on v4

--- a/solution.py
+++ b/solution.py
@@ -23,8 +23,9 @@
 PACK_EARLY = 2
 SENT_FIRST = 2
 PACK_PAIR = 4
-SENT_SECOND = 8
-SRC_EARLY = 0
+SRC_NOW = 4
+SRC_MID = 8
+MID_AT = 7
 STEP = 2
 LAST = 2
 VLIM = 56 << 20
@@ -249,12 +250,9 @@
         send_tgt(g)
     for i in range(PACK_PAIR, NGROUP):
         pack_tgt(GROUPS[i])
-        if i < SENT_SECOND:
-            send_tgt(GROUPS[i])
-    for i, g in enumerate(GROUPS):
+        send_tgt(GROUPS[i])
+    for g in GROUPS:
         pack_src(g)
-        if i < SRC_EARLY:
-            send_src(g)
 
     rest = rr.at[pl.ds(1, 63)]
     remote(rest, rest, rs_s, rs_r, partner).wait_recv()
@@ -269,9 +267,7 @@
     for kc in chips:
         ds, dz = kc // 4, kc % 4
         remote(mine, mine, ag_s, ag_r, (sx[ds], tx[dz * 2])).start()
-    for g in GROUPS[SENT_SECOND:]:
-        send_tgt(g)
-    for g in GROUPS[SRC_EARLY:]:
+    for g in GROUPS[:SRC_NOW]:
         send_src(g)
 
     def owner_tgt(g):
@@ -284,15 +280,18 @@
         sfall[to, :] = jnp.concatenate([facs[0:64], facs[64:128]], axis=1)
         tfall[to, :] = jnp.concatenate([facs[128:192], facs[192:256]], axis=1)
 
-    for g in GROUPS[:SENT_SECOND]:
+    for i, g in enumerate(GROUPS):
         owner_tgt(g)
+        if i == MID_AT:
+            for h in GROUPS[SRC_NOW:SRC_MID]:
+                send_src(h)
 
     remote(rest, rest, ag_s, ag_r, partner).wait_recv()
     pair_back = remote(mm.at[core], mm.at[core], pb_s, pb_r, partner)
     pair_back.start()
 
-    for g in GROUPS[SENT_SECOND:]:
-        owner_tgt(g)
+    for g in GROUPS[SRC_MID:]:
+        send_src(g)
 
     def squares_of(points):
         total = jnp.zeros((points.shape[0], 128), F32)

time: 71.9 us -> 71.9 us (level)
  no operation moved by 1% of the time
where the time goes in v5:
time: 71.9 us; the launch traced here: 71.7 us
  Pallas kernels  70.9 us (99%)
  between operations  0.8 us (1%)
    pallas_call x1, Pallas kernels, per_device(): pl.pallas_call(kernel, out_shape=(pltpu.VMEM((ROWS, R), BF), pltpu.VMEM((...  70 us

profile of v5, /device:TPU:1, one launch (start us, length us, event | category | flops | bytes accessed | tf_op | source)
XLA Modules:
  0.0 71.7 jit_solution(13471745600113610003)
XLA Ops:
  0.6 70.0 %transport.1 = (bf16[256,256]{1,0:T(8,128)(2,1)S(1)}, bf16[256,256]{1,0:T(8,128)(2,1)S(1)}, bf16[256,1024]{1,0:T(8,128)(2,1)S(1)}) custom-call(bf16[256,1024]{1,0:T(8,128)(2,1)} %sp_in.1, bf16[256,1024]{1,0:T(8,128)(2,1)} %tp_in.1, bf16[256,256]{1,0:T(8,128)(2,1)} %sf_in.1, bf16[256,256]{1,0:T(8,128)(2,1)} %tf_in.1, f32[1,256]{1,0:T(1,128)} %bitcast.3, ...), custom_call_target="tpu_custom_call" | custom-call | tf_op jit(solution)/shard_map/transport/pallas_call | solution.py:391
  70.7 0.9 %put_out.1 = (bf16[256,256]{1,0:T(8,128)(2,1)}, bf16[256,256]{1,0:T(8,128)(2,1)}, bf16[256,1024]{1,0:T(8,128)(2,1)}) custom-call(bf16[256,256]{1,0:T(8,128)(2,1)S(1)} %get-tuple-element.6.su, bf16[256,256]{1,0:T(8,128)(2,1)S(1)} %get-tuple-element.7.tu, bf16[256,1024]{1,0:T(8,128)(2,1)S(1)} %get-tuple-element.8.mp), custom_call_target="tpu_custom_call" | custom-call | tf_op jit(solution)/shard_map/put_out/pallas_call | solution.py:439
